TPU v7x, 512 devices: a whole 4x8x8 slice. The times are simulated.
512 devices in a mesh: seg: 4 (over y_hi, core), pan: 128 (over y_lo, z, x).
Axes of the slice: x: 4, y: 8 (y_hi: 2, y_lo: 4; y = y_hi * 4 + y_lo), z: 8, core: 2. Of those that a mesh axis runs over, the one named last changes fastest.
Arguments:
- sources: bfloat16 [2, 2, 64, 1048576], P(None, None, 'seg', 'pan'), may hold values from -0.75 to 0.75
- panel_geom: float32 [6, 1048576], P(None, 'pan'), may hold values from -1 to 1, as said below
- mic_pos: float32 [3, 1024], replicated, may hold values from -12 to 12, as said below
- mic_order: int32 [1024], replicated, may hold values from 0 to 1023, each once
Outputs:
- csm: float32 [2, 1024, 1024], P(None, 'pan', 'seg')
Inputs may be any that keep to these rules, and one draw needn't show every extreme that they name: `mic_order`: each of the 1024 microphones stands exactly once. `panel_geom`: panel centres lie on a cylinder of radius 1 around the first axis with first coordinate within -1 to 1; normals are the unit radial directions. `mic_pos`: microphones lie at distances 6 to 12 from the anchor (0, 0, 0).
All inputs are finite; a program needn't handle non-finite values.
Results may differ from a plain program's by a relative error of at most 0.0039.
Values may be sent and summed in bfloat16 or wider, within the bound.
No kernel may reach another device: no remote copies, remote signals or barrier semaphores. Data moves between devices by JAX's collectives and lax.ppermute only.
A program may use at most 64 MiB of HBM per device.

v0:
```python
import math
import jax
import jax.numpy as jnp
from jax import lax
from jax.sharding import PartitionSpec as P

mach_number = 0.3
beta_sq = 0.91
wave_number = 40.0


def kernel_block(mics, geometry):
    dx = mics[0][:, None] - geometry[0][None, :]
    dy = mics[1][:, None] - geometry[1][None, :]
    dz = mics[2][:, None] - geometry[2][None, :]
    rstar = jnp.sqrt(dx * dx + beta_sq * (dy * dy + dz * dz))
    radius = (rstar - mach_number * dx) / beta_sq
    phase = wave_number * radius
    amplitude = 1.0 / (4.0 * math.pi * rstar)
    green_re = amplitude * jnp.cos(phase)
    green_im = -amplitude * jnp.sin(phase)
    normal_part = (
        dx * geometry[3][None, :] + dy * geometry[4][None, :] + dz * geometry[5][None, :]
    ) / rstar
    scale_re = normal_part / (wave_number * rstar)
    dip_re = scale_re * green_re - normal_part * green_im
    dip_im = scale_re * green_im + normal_part * green_re
    return jnp.concatenate([green_re, green_im, dip_re, dip_im], axis=1).astype(jnp.bfloat16)


def block_weights(piece):
    swapped = jnp.transpose(piece, (0, 1, 3, 2))
    real_cols = jnp.concatenate(
        [swapped[0, 0], -swapped[1, 0], swapped[0, 1], -swapped[1, 1]], axis=0
    )
    imag_cols = jnp.concatenate(
        [swapped[1, 0], swapped[0, 0], swapped[1, 1], swapped[0, 1]], axis=0
    )
    return jnp.concatenate([real_cols, imag_cols], axis=1)


def split_sources(sources, blocks, block_size):
    shaped = sources.reshape(2, 2, sources.shape[2], blocks, block_size)
    return jnp.transpose(shaped, (3, 0, 1, 2, 4))


def panel_spectra(mics, geom_blocks, source_blocks):

    def step(running, pair):
        geometry, piece = pair
        weights = block_weights(piece)
        return (
            running
            + jnp.dot(kernel_block(mics, geometry), weights, preferred_element_type=jnp.float32),
            None,
        )

    init = jnp.zeros((mics.shape[1], 2 * source_blocks.shape[3]), jnp.float32)
    summed, unused = lax.scan(step, init, (geom_blocks, source_blocks))
    return summed


def summed_spectra(mic_rows, geom_blocks, source_blocks):
    local_terms = panel_spectra(mic_rows, geom_blocks, source_blocks)
    return lax.psum(local_terms, "pan")


def cross_terms(own_rows, columns):
    half = columns.shape[1] // 2
    rows_re = own_rows[:, :half]
    rows_im = own_rows[:, half:]
    cols_re = columns[:, :half]
    cols_im = columns[:, half:]
    highest = lax.Precision.HIGHEST
    csm_re = jnp.dot(rows_re, cols_re.T, precision=highest) + jnp.dot(
        rows_im, cols_im.T, precision=highest
    )
    csm_im = jnp.dot(rows_im, cols_re.T, precision=highest) - jnp.dot(
        rows_re, cols_im.T, precision=highest
    )
    return jnp.stack([csm_re, csm_im])


def shards(sources, panel_geom, mic_pos, mic_order):
    ordered = jnp.take(mic_pos, mic_order, axis=1)
    panels_here = panel_geom.shape[1]
    block_size = min(512, panels_here)
    blocks = panels_here // block_size
    geom_blocks = jnp.transpose(panel_geom.reshape(6, blocks, block_size), (1, 0, 2))
    mics_all = ordered.shape[1]
    seg_count = lax.axis_size("seg")
    row_count = mics_all // lax.axis_size("pan")
    row_start = lax.axis_index("pan") * row_count
    source_blocks = split_sources(sources, blocks, block_size)
    spectra = summed_spectra(ordered, geom_blocks, source_blocks)
    own_rows = lax.dynamic_slice_in_dim(spectra, row_start, row_count, 0)
    partial_csm = cross_terms(own_rows, spectra)
    summed = lax.psum_scatter(partial_csm, "seg", scatter_dimension=2, tiled=True)
    return summed / (own_rows.shape[1] // 2 * seg_count)


def solution(mesh):
    placed = (P(None, None, "seg", "pan"), P(None, "pan"), P(), P())
    return jax.shard_map(
        shards, mesh=mesh, in_specs=placed, out_specs=P(None, "pan", "seg"), check_vma=False
    )
```

profile of v0, /device:TPU:1, one launch (start us, length us, event | category | flops | bytes accessed | tf_op | source)
XLA Modules:
  0.0 1561.1 jit_solution(7481023906343510673)
XLA Ops:
  7.9 1.0 copy.7
  9.0 2.8 gather_fusion
  12.5 1.5 copy.9
  14.1 267.6 %while.13 = (s32[]{:T(128)}, f32[1024,32]{0,1:T(8,128)S(1)}, f32[3,1024]{1,0:T(4,128)S(1)}, f32[16,6,512]{2,1,0:T(8,128)}, bf16[16,2,2,16,512]{4,3,2,1,0:T(8,128...) while((s32[]{:T(128)}, f32[1024,32]{0,1:T(8,128)S(1)}, ...), condition=%wide.region_1.2_spmd.clone, body=%wide.region_0.1_spmd.clone.sunk | while | flops 170999808 | bytes 9150687 | solution.py:59
  15.1 12.3 subtract_convert_fusion.2
  28.2 2.6 fusion.66
  30.8 1.0 constant_dynamic-slice_fusion.7
  31.8 12.3 subtract_convert_fusion.2
  44.9 2.6 fusion.66
  47.5 1.0 constant_dynamic-slice_fusion.7
  48.5 12.3 subtract_convert_fusion.2
  61.6 2.6 fusion.66
  64.2 1.0 constant_dynamic-slice_fusion.7
  65.2 12.3 subtract_convert_fusion.2
  78.4 2.6 fusion.66
  81.0 1.0 constant_dynamic-slice_fusion.7
  81.9 12.3 subtract_convert_fusion.2
  95.1 2.6 fusion.66
  97.7 1.0 constant_dynamic-slice_fusion.7
  98.7 12.3 subtract_convert_fusion.2
  111.8 2.6 fusion.66
  115.4 12.3 subtract_convert_fusion.2
  128.5 2.6 fusion.66
  132.1 12.3 subtract_convert_fusion.2
  145.3 2.6 fusion.66
  148.8 12.3 subtract_convert_fusion.2
  162.0 2.6 fusion.66
  165.6 12.3 subtract_convert_fusion.2
  178.7 2.6 fusion.66
  182.3 12.3 subtract_convert_fusion.2
  195.4 2.6 fusion.66
  199.0 12.3 subtract_convert_fusion.2
  212.2 2.6 fusion.66
  215.7 12.3 subtract_convert_fusion.2
  228.9 2.6 fusion.66
  232.5 12.3 subtract_convert_fusion.2
  245.6 2.6 fusion.66
  249.2 12.3 subtract_convert_fusion.2
  262.3 2.6 fusion.66
  265.9 12.3 subtract_convert_fusion.2
  279.1 2.6 fusion.66
  282.4 1203.3 %all-reduce.2.cloned.1.call-done = f32[1024,32]{0,1:T(8,128)} async-done(((f32[1024,32]{0,1:T(8,128)}), f32[1024,32]{0,1:T(8,128)}) %all-reduce.2.cloned.1.call-update) | async-done | bytes 131088 | tf_op jit(solution)/shard_map/psum | solution.py:65
  1485.7 1.2 fusion.47
  1486.9 1.2 fusion.45
  1488.1 1.2 fusion.41
  1489.2 1.2 fusion.42
  1491.1 61.8 %reduce-scatter.2.cloned.1.call-done = f32[2,8,256]{2,1,0:T(8,128)} async-done(((f32[2,8,1024]{2,1,0:T(8,128)}), f32[2,8,256]{2,1,0:T(8,128)}) %reduce-scatter.2.cloned.1.call-update) | async-done | bytes 16400 | tf_op jit(solution)/shard_map/reduce_scatter | solution.py:98
  1552.9 1.3 broadcast_multiply_fusion
  (90 shorter events, 28.0 us)
Async XLA Ops:
  6.5 1479.1 %all-reduce.2.cloned.1.call-start = ((), (), s32[]{:S(2)}) async-start(), calls=%async_computation.1 | async-start | bytes 262144 | tf_op jit(solution)/shard_map/psum | solution.py:65
  7.9 4.2 copy-start
  281.6 0.7 copy-start.1
  282.3 1270.6 %reduce-scatter.2.cloned.1.call-start = ((), (), s32[]{:S(2)}) async-start(), calls=%async_computation.2 | async-start | bytes 81920 | tf_op jit(solution)/shard_map/reduce_scatter | solution.py:98
Sparse Core Ops, SparseCore 0:
  282.4 1203.1 all-reduce.1
  1491.2 61.6 reduce-scatter.1
where the time goes:
time: 1560 us
  waiting for transfers between devices  1270 us (81%)
  other arithmetic  200 us (13%)
  matrix products  45.8 us (3%)
  local copies, waits for them, and re-layouts  35.8 us (2%)
    psum x1, waiting for transfers between devices, summed_spectra(): return lax.psum(local_terms, 'pan')  1200 us
    another operation x16, other arithmetic  196 us
    reduce_scatter x1, waiting for transfers between devices, shards(): lax.psum_scatter(partial_csm, 'seg', scatter_dimension=2, tiled=True)  61.8 us
    dot_general x16, matrix products, step(): jnp.dot(kernel_block(mics, geometry), weights, preferred_element_type=jnp...  41.1 us
  transfers between devices with their start and end apart: 2, of which 2 were waited for; matrix products, arithmetic and copies ran while one was open for 0% of the time, Pallas kernels for 0%

commit v1 on v0

--- a/solution.py
+++ b/solution.py
@@ -62,7 +62,8 @@
 
 def summed_spectra(mic_rows, geom_blocks, source_blocks):
     local_terms = panel_spectra(mic_rows, geom_blocks, source_blocks)
-    return lax.psum(local_terms, "pan")
+    samples_all_bring = lambda inputs, chip_axis: jnp.sum(lax.all_gather(inputs, chip_axis), axis=0)
+    return samples_all_bring(local_terms, "pan")
 
 
 def cross_terms(own_rows, columns):

time: 1560 us -> 1080 us (0.69)
  waiting for transfers between devices: 1270 us -> 756 us
  local copies, waits for them, and re-layouts: 35.8 us -> 53.4 us
    psum x1 -> x0, waiting for transfers between devices: 1200 us -> none  [summed_spectra(): return lax.psum(local_terms, 'pan')]
    all_gather x0 -> x1, waiting for transfers between devices: none -> 647 us  [summed_spectra(): lax.all_gather(inputs, chip_axis)]
    reduce_scatter x1, waiting for transfers between devices: 61.8 us -> 109 us  [shards(): lax.psum_scatter(partial_csm, 'seg', scatter_dimension=2, tiled=True)]
    unnamed x8 -> x9, local copies, waits for them, and re-layouts: 3.77 us -> 21.3 us
where the time goes in v1:
time: 1080 us; the launch traced here: 1070 us
  waiting for transfers between devices  756 us (70%)
  other arithmetic  208 us (19%)
  local copies, waits for them, and re-layouts  53.4 us (5%)
  matrix products  42.3 us (4%)
  between operations  13.5 us (1%)
    all_gather x1, waiting for transfers between devices, summed_spectra(): lax.all_gather(inputs, chip_axis)  647 us
    another operation x16, other arithmetic  196 us
    reduce_scatter x1, waiting for transfers between devices, shards(): lax.psum_scatter(partial_csm, 'seg', scatter_dimension=2, tiled=True)  109 us
    dot_general x16, matrix products, step(): jnp.dot(kernel_block(mics, geometry), weights, preferred_element_type=jnp...  41.1 us
  transfers between devices with their start and end apart: 2, of which 2 were waited for; matrix products, arithmetic and copies ran while one was open for 0% of the time, Pallas kernels for 0%

profile of v1, /device:TPU:1, one launch (start us, length us, event | category | flops | bytes accessed | tf_op | source)
XLA Modules:
  0.0 1074.4 jit_solution(11307290253005227977)
XLA Ops:
  9.0 2.8 gather_fusion
  12.5 1.5 copy.12
  14.1 267.6 %while.13 = (s32[]{:T(128)}, f32[1024,32]{0,1:T(8,128)S(1)}, f32[3,1024]{1,0:T(4,128)S(1)}, f32[16,6,512]{2,1,0:T(8,128)}, bf16[16,2,2,16,512]{4,3,2,1,0:T(8,128...) while((s32[]{:T(128)}, f32[1024,32]{0,1:T(8,128)S(1)}, ...), condition=%wide.region_1.2_spmd.clone, body=%wide.region_0.1_spmd.clone.sunk | while | flops 170999808 | bytes 9150687 | solution.py:59
  15.1 12.3 %subtract_convert_fusion.2 = (bf16[1024,512]{1,0:T(8,128)(2,1)S(1)}, bf16[1024,512]{1,0:T(8,128)(2,1)S(1)}, bf16[1024,512]{1,0:T(8,128)(2,1)S(1)}, bf16[1024,512]{1,0:T(8,128)(2,1)}) fusion(f32[512]{0:T(512)S(1)} %bitcast.81, f32[512]{0:T(512)S(1)} %bitcast.79, f32[1024]{0:T(1024)S(1)} %bitcast.74, f32[512]{0:T(512)S(1)} %bitcast.77, ...), kind=kLoop, calls=%fused_computation.28.clone.1 | loop fusion | flops 18874368 | bytes 4218880 | tf_op jit(solution)/shard_map/convert.2
  28.2 2.6 fusion.66
  30.8 1.0 constant_dynamic-slice_fusion.7
  31.8 12.3 %subtract_convert_fusion.2 = (bf16[1024,512]{1,0:T(8,128)(2,1)S(1)}, bf16[1024,512]{1,0:T(8,128)(2,1)S(1)}, bf16[1024,512]{1,0:T(8,128)(2,1)S(1)}, bf16[1024,512]{1,0:T(8,128)(2,1)}) fusion(f32[512]{0:T(512)S(1)} %bitcast.81, f32[512]{0:T(512)S(1)} %bitcast.79, f32[1024]{0:T(1024)S(1)} %bitcast.74, f32[512]{0:T(512)S(1)} %bitcast.77, ...), kind=kLoop, calls=%fused_computation.28.clone.1 | loop fusion | flops 18874368 | bytes 4218880 | tf_op jit(solution)/shard_map/convert.2
  44.9 2.6 fusion.66
  47.5 1.0 constant_dynamic-slice_fusion.7
  48.5 12.3 %subtract_convert_fusion.2 = (bf16[1024,512]{1,0:T(8,128)(2,1)S(1)}, bf16[1024,512]{1,0:T(8,128)(2,1)S(1)}, bf16[1024,512]{1,0:T(8,128)(2,1)S(1)}, bf16[1024,512]{1,0:T(8,128)(2,1)}) fusion(f32[512]{0:T(512)S(1)} %bitcast.81, f32[512]{0:T(512)S(1)} %bitcast.79, f32[1024]{0:T(1024)S(1)} %bitcast.74, f32[512]{0:T(512)S(1)} %bitcast.77, ...), kind=kLoop, calls=%fused_computation.28.clone.1 | loop fusion | flops 18874368 | bytes 4218880 | tf_op jit(solution)/shard_map/convert.2
  61.6 2.6 fusion.66
  64.2 1.1 constant_dynamic-slice_fusion.7
  65.3 12.3 %subtract_convert_fusion.2 = (bf16[1024,512]{1,0:T(8,128)(2,1)S(1)}, bf16[1024,512]{1,0:T(8,128)(2,1)S(1)}, bf16[1024,512]{1,0:T(8,128)(2,1)S(1)}, bf16[1024,512]{1,0:T(8,128)(2,1)}) fusion(f32[512]{0:T(512)S(1)} %bitcast.81, f32[512]{0:T(512)S(1)} %bitcast.79, f32[1024]{0:T(1024)S(1)} %bitcast.74, f32[512]{0:T(512)S(1)} %bitcast.77, ...), kind=kLoop, calls=%fused_computation.28.clone.1 | loop fusion | flops 18874368 | bytes 4218880 | tf_op jit(solution)/shard_map/convert.2
  78.5 2.6 fusion.66
  81.1 1.0 constant_dynamic-slice_fusion.7
  82.0 12.3 %subtract_convert_fusion.2 = (bf16[1024,512]{1,0:T(8,128)(2,1)S(1)}, bf16[1024,512]{1,0:T(8,128)(2,1)S(1)}, bf16[1024,512]{1,0:T(8,128)(2,1)S(1)}, bf16[1024,512]{1,0:T(8,128)(2,1)}) fusion(f32[512]{0:T(512)S(1)} %bitcast.81, f32[512]{0:T(512)S(1)} %bitcast.79, f32[1024]{0:T(1024)S(1)} %bitcast.74, f32[512]{0:T(512)S(1)} %bitcast.77, ...), kind=kLoop, calls=%fused_computation.28.clone.1 | loop fusion | flops 18874368 | bytes 4218880 | tf_op jit(solution)/shard_map/convert.2
  95.2 2.6 fusion.66
  98.8 12.3 %subtract_convert_fusion.2 = (bf16[1024,512]{1,0:T(8,128)(2,1)S(1)}, bf16[1024,512]{1,0:T(8,128)(2,1)S(1)}, bf16[1024,512]{1,0:T(8,128)(2,1)S(1)}, bf16[1024,512]{1,0:T(8,128)(2,1)}) fusion(f32[512]{0:T(512)S(1)} %bitcast.81, f32[512]{0:T(512)S(1)} %bitcast.79, f32[1024]{0:T(1024)S(1)} %bitcast.74, f32[512]{0:T(512)S(1)} %bitcast.77, ...), kind=kLoop, calls=%fused_computation.28.clone.1 | loop fusion | flops 18874368 | bytes 4218880 | tf_op jit(solution)/shard_map/convert.2
  111.9 2.6 fusion.66
  114.5 1.0 constant_dynamic-slice_fusion.7
  115.5 12.3 %subtract_convert_fusion.2 = (bf16[1024,512]{1,0:T(8,128)(2,1)S(1)}, bf16[1024,512]{1,0:T(8,128)(2,1)S(1)}, bf16[1024,512]{1,0:T(8,128)(2,1)S(1)}, bf16[1024,512]{1,0:T(8,128)(2,1)}) fusion(f32[512]{0:T(512)S(1)} %bitcast.81, f32[512]{0:T(512)S(1)} %bitcast.79, f32[1024]{0:T(1024)S(1)} %bitcast.74, f32[512]{0:T(512)S(1)} %bitcast.77, ...), kind=kLoop, calls=%fused_computation.28.clone.1 | loop fusion | flops 18874368 | bytes 4218880 | tf_op jit(solution)/shard_map/convert.2
  128.6 2.6 fusion.66
  132.2 12.3 %subtract_convert_fusion.2 = (bf16[1024,512]{1,0:T(8,128)(2,1)S(1)}, bf16[1024,512]{1,0:T(8,128)(2,1)S(1)}, bf16[1024,512]{1,0:T(8,128)(2,1)S(1)}, bf16[1024,512]{1,0:T(8,128)(2,1)}) fusion(f32[512]{0:T(512)S(1)} %bitcast.81, f32[512]{0:T(512)S(1)} %bitcast.79, f32[1024]{0:T(1024)S(1)} %bitcast.74, f32[512]{0:T(512)S(1)} %bitcast.77, ...), kind=kLoop, calls=%fused_computation.28.clone.1 | loop fusion | flops 18874368 | bytes 4218880 | tf_op jit(solution)/shard_map/convert.2
  145.4 2.6 fusion.66
  147.9 1.0 constant_dynamic-slice_fusion.7
  148.9 12.3 %subtract_convert_fusion.2 = (bf16[1024,512]{1,0:T(8,128)(2,1)S(1)}, bf16[1024,512]{1,0:T(8,128)(2,1)S(1)}, bf16[1024,512]{1,0:T(8,128)(2,1)S(1)}, bf16[1024,512]{1,0:T(8,128)(2,1)}) fusion(f32[512]{0:T(512)S(1)} %bitcast.81, f32[512]{0:T(512)S(1)} %bitcast.79, f32[1024]{0:T(1024)S(1)} %bitcast.74, f32[512]{0:T(512)S(1)} %bitcast.77, ...), kind=kLoop, calls=%fused_computation.28.clone.1 | loop fusion | flops 18874368 | bytes 4218880 | tf_op jit(solution)/shard_map/convert.2
  162.1 2.6 fusion.66
  165.7 12.3 %subtract_convert_fusion.2 = (bf16[1024,512]{1,0:T(8,128)(2,1)S(1)}, bf16[1024,512]{1,0:T(8,128)(2,1)S(1)}, bf16[1024,512]{1,0:T(8,128)(2,1)S(1)}, bf16[1024,512]{1,0:T(8,128)(2,1)}) fusion(f32[512]{0:T(512)S(1)} %bitcast.81, f32[512]{0:T(512)S(1)} %bitcast.79, f32[1024]{0:T(1024)S(1)} %bitcast.74, f32[512]{0:T(512)S(1)} %bitcast.77, ...), kind=kLoop, calls=%fused_computation.28.clone.1 | loop fusion | flops 18874368 | bytes 4218880 | tf_op jit(solution)/shard_map/convert.2
  178.8 2.6 fusion.66
  181.4 1.0 constant_dynamic-slice_fusion.7
  182.4 12.3 %subtract_convert_fusion.2 = (bf16[1024,512]{1,0:T(8,128)(2,1)S(1)}, bf16[1024,512]{1,0:T(8,128)(2,1)S(1)}, bf16[1024,512]{1,0:T(8,128)(2,1)S(1)}, bf16[1024,512]{1,0:T(8,128)(2,1)}) fusion(f32[512]{0:T(512)S(1)} %bitcast.81, f32[512]{0:T(512)S(1)} %bitcast.79, f32[1024]{0:T(1024)S(1)} %bitcast.74, f32[512]{0:T(512)S(1)} %bitcast.77, ...), kind=kLoop, calls=%fused_computation.28.clone.1 | loop fusion | flops 18874368 | bytes 4218880 | tf_op jit(solution)/shard_map/convert.2
  195.5 2.6 fusion.66
  199.1 12.3 %subtract_convert_fusion.2 = (bf16[1024,512]{1,0:T(8,128)(2,1)S(1)}, bf16[1024,512]{1,0:T(8,128)(2,1)S(1)}, bf16[1024,512]{1,0:T(8,128)(2,1)S(1)}, bf16[1024,512]{1,0:T(8,128)(2,1)}) fusion(f32[512]{0:T(512)S(1)} %bitcast.81, f32[512]{0:T(512)S(1)} %bitcast.79, f32[1024]{0:T(1024)S(1)} %bitcast.74, f32[512]{0:T(512)S(1)} %bitcast.77, ...), kind=kLoop, calls=%fused_computation.28.clone.1 | loop fusion | flops 18874368 | bytes 4218880 | tf_op jit(solution)/shard_map/convert.2
  212.3 2.6 fusion.66
  214.8 1.0 constant_dynamic-slice_fusion.7
  215.8 12.3 %subtract_convert_fusion.2 = (bf16[1024,512]{1,0:T(8,128)(2,1)S(1)}, bf16[1024,512]{1,0:T(8,128)(2,1)S(1)}, bf16[1024,512]{1,0:T(8,128)(2,1)S(1)}, bf16[1024,512]{1,0:T(8,128)(2,1)}) fusion(f32[512]{0:T(512)S(1)} %bitcast.81, f32[512]{0:T(512)S(1)} %bitcast.79, f32[1024]{0:T(1024)S(1)} %bitcast.74, f32[512]{0:T(512)S(1)} %bitcast.77, ...), kind=kLoop, calls=%fused_computation.28.clone.1 | loop fusion | flops 18874368 | bytes 4218880 | tf_op jit(solution)/shard_map/convert.2
  229.0 2.6 fusion.66
  232.6 12.3 %subtract_convert_fusion.2 = (bf16[1024,512]{1,0:T(8,128)(2,1)S(1)}, bf16[1024,512]{1,0:T(8,128)(2,1)S(1)}, bf16[1024,512]{1,0:T(8,128)(2,1)S(1)}, bf16[1024,512]{1,0:T(8,128)(2,1)}) fusion(f32[512]{0:T(512)S(1)} %bitcast.81, f32[512]{0:T(512)S(1)} %bitcast.79, f32[1024]{0:T(1024)S(1)} %bitcast.74, f32[512]{0:T(512)S(1)} %bitcast.77, ...), kind=kLoop, calls=%fused_computation.28.clone.1 | loop fusion | flops 18874368 | bytes 4218880 | tf_op jit(solution)/shard_map/convert.2
  245.7 2.6 fusion.66
  249.3 12.3 %subtract_convert_fusion.2 = (bf16[1024,512]{1,0:T(8,128)(2,1)S(1)}, bf16[1024,512]{1,0:T(8,128)(2,1)S(1)}, bf16[1024,512]{1,0:T(8,128)(2,1)S(1)}, bf16[1024,512]{1,0:T(8,128)(2,1)}) fusion(f32[512]{0:T(512)S(1)} %bitcast.81, f32[512]{0:T(512)S(1)} %bitcast.79, f32[1024]{0:T(1024)S(1)} %bitcast.74, f32[512]{0:T(512)S(1)} %bitcast.77, ...), kind=kLoop, calls=%fused_computation.28.clone.1 | loop fusion | flops 18874368 | bytes 4218880 | tf_op jit(solution)/shard_map/convert.2
  262.4 2.6 fusion.66
  266.0 12.3 %subtract_convert_fusion.2 = (bf16[1024,512]{1,0:T(8,128)(2,1)S(1)}, bf16[1024,512]{1,0:T(8,128)(2,1)S(1)}, bf16[1024,512]{1,0:T(8,128)(2,1)S(1)}, bf16[1024,512]{1,0:T(8,128)(2,1)}) fusion(f32[512]{0:T(512)S(1)} %bitcast.81, f32[512]{0:T(512)S(1)} %bitcast.79, f32[1024]{0:T(1024)S(1)} %bitcast.74, f32[512]{0:T(512)S(1)} %bitcast.77, ...), kind=kLoop, calls=%fused_computation.28.clone.1 | loop fusion | flops 18874368 | bytes 4218880 | tf_op jit(solution)/shard_map/convert.2
  279.2 2.6 fusion.66
  282.5 647.1 %all-gather.3.cloned.1.call-done = f32[131072,32]{0,1:T(8,128)} async-done(((f32[1024,32]{0,1:T(8,128)}), f32[131072,32]{0,1:T(8,128)}) %all-gather.3.cloned.1.call-update) | async-done | bytes 16777232 | tf_op jit(solution)/shard_map/all_gather | solution.py:65
  929.6 17.7 %copy.14 = f32[4,8,128,1024]{3,2,1,0:T(8,128)} copy(f32[4,8,128,1024]{3,1,2,0:T(8,128)} %bitcast.70) | data formatting | bytes 33554432
  947.2 8.1 bitcast_reduce_fusion
  957.2 109.1 %reduce-scatter.2.cloned.1.call-done = f32[2,8,256]{2,1,0:T(8,128)} async-done(((f32[2,8,1024]{2,1,0:T(8,128)}), f32[2,8,256]{2,1,0:T(8,128)}) %reduce-scatter.2.cloned.1.call-update) | async-done | bytes 16400 | tf_op jit(solution)/shard_map/reduce_scatter | solution.py:99
  1066.3 1.3 broadcast_multiply_fusion
  (92 shorter events, 27.3 us)
Async XLA Ops:
  6.5 5.6 copy-start
  6.5 923.0 %all-gather.3.cloned.1.call-start = ((), (), s32[]{:S(2)}) async-start(), calls=%async_computation.2 | async-start | bytes 16908288 | tf_op jit(solution)/shard_map/all_gather | solution.py:65
  281.7 0.7 copy-start.1
  282.4 783.8 %reduce-scatter.2.cloned.1.call-start = ((), (), s32[]{:S(2)}) async-start(), calls=%async_computation.1 | async-start | bytes 81920 | tf_op jit(solution)/shard_map/reduce_scatter | solution.py:99
Sparse Core Ops, SparseCore 0:
  282.5 646.9 all-gather.2
  957.3 108.9 reduce-scatter.1
